TPU v7x, 256 devices: a whole 4x4x8 slice. The times are simulated.
256 devices in a mesh: grp: 8 (over x, core), dev: 32 (over y, z).
Axes of the slice: x: 4, y: 4, z: 8, core: 2. Of those that a mesh axis runs over, the one named last changes fastest.
Arguments:
- queries: bfloat16 [65536, 768], P(('grp', 'dev')), may hold values from -1.796875 to 1.796875
- query_slots: int32 [65536], P('grp'), may hold values from 0 to 8191, as said below
- w_res: bfloat16 [768, 768], replicated, may hold values from -0.21875 to 0.21875
- labels: bfloat16 [5120, 128, 768], P(('grp', 'dev')), may hold values from -0.71875 to 0.71875
- blocks: int32 [512, 12], P('grp'), may hold values from 0 to 5119, as said below
- positives: int32 [65536, 4], P(('grp', 'dev')), may hold values from 0 to 655359, as said below
Outputs:
- query_loss: float32 [65536], P(('grp', 'dev'))
- query_grad: bfloat16 [65536, 768], P(('grp', 'dev'))
- label_grad: bfloat16 [5120, 128, 768], P(('grp', 'dev'))
- residual_grad: bfloat16 [768, 768], replicated
Inputs may be any that keep to these rules, and one draw needn't show every extreme that they name: `query_slots`: the rows of one grp index (rows g * 256 * 32 onward) hold a permutation of 0 to 8191; a place // 256 is the dev index that owns the query's cluster, and the 256 rows of every device send exactly 8 queries to each owner. Row c lists 12 different blocks, all held by devices of the same grp index as the cluster's owner (device c // 2). The 2 clusters of one device list at most 16 distinct blocks, of which at most 1 are held by any one device; for every device's clusters some holder reaches 1. `positives`: the 4 labels of row r are different and lie in 4 different blocks listed for cluster r // 128.
All inputs are finite; a program needn't handle non-finite values.
Results may differ from a plain program's by a relative error of at most 0.0047.
The roundings to bfloat16 on the way count: a program that leaves them out, or rounds other values in their place, can miss the bound.
Values may be sent and summed in bfloat16 or wider, within the bound.
No kernel may reach another device: no remote copies, remote signals or barrier semaphores. Data moves between devices by JAX's collectives and lax.ppermute only.
A program may use at most 128 MiB of HBM per device.

v0:
```python
from functools import partial
import jax
import jax.numpy as jnp
from jax import lax
from jax.sharding import PartitionSpec as P

BLK = 128
CSIZE = 128
SHORT = 12
NPOS = 4
POOL = 16
BLK_DEV = 20


def activate(values):
    return jax.nn.gelu(values, approximate=True)


def activate_slope(values):
    return jax.vjp(activate, values)[1](jnp.ones_like(values))[0]


def request_plan(listed, owner_base, peer_count, per_owner):
    owners = listed // BLK_DEV - owner_base
    within = listed % BLK_DEV
    positions = jnp.arange(listed.shape[0], dtype=jnp.int32)
    earlier = positions[None, :] < positions[:, None]
    same_block = listed[:, None] == listed[None, :]
    leading = jnp.logical_not(jnp.any(same_block & earlier, axis=1))
    first_seen = jnp.argmax(same_block, axis=1)
    same_owner = owners[:, None] == owners[None, :]
    ranking = jnp.sum(same_owner & earlier & leading[None, :], axis=1)
    own_place = owners * per_owner + ranking
    placed = own_place[first_seen]
    target = jnp.where(leading, own_place, peer_count * per_owner)
    request_table = (
        jnp.full((peer_count * per_owner,), -1, jnp.int32).at[target].set(within, mode="drop")
    )
    return (placed, request_table.reshape(peer_count, per_owner))


def local(queries, query_slots, w_res, labels, blocks, positives):
    peer_count = lax.axis_size("dev")
    groups = lax.axis_size("grp")
    own_index = lax.axis_index("dev")
    group_index = lax.axis_index("grp")
    rows_dev = queries.shape[0]
    feature_width = queries.shape[1]
    per_peer = rows_dev // peer_count
    clusters_dev = rows_dev // CSIZE
    per_owner = (POOL + peer_count - 1) // peer_count
    slots_total = peer_count * per_owner
    own_slots = lax.dynamic_slice_in_dim(query_slots, own_index * rows_dev, rows_dev)
    outbound = jnp.argsort(own_slots // rows_dev, stable=True)
    slot_grid = query_slots.reshape(peer_count, rows_dev)
    grid_order = jnp.argsort(slot_grid // rows_dev, axis=1, stable=True)
    grid_sorted = jnp.take_along_axis(slot_grid, grid_order, axis=1)
    incoming = (
        lax.dynamic_slice_in_dim(grid_sorted, own_index * per_peer, per_peer, 1).reshape(rows_dev)
        - own_index * rows_dev
    )
    arrange = jnp.argsort(incoming)
    pre_act = jnp.dot(queries, w_res, preferred_element_type=jnp.float32)
    payload = (queries.astype(jnp.float32) + activate(pre_act)).astype(jnp.bfloat16)
    arrived = lax.all_to_all(
        payload[outbound].reshape(peer_count, per_peer, feature_width),
        "dev",
        split_axis=0,
        concat_axis=0,
        tiled=True,
    )
    arrived = arrived.reshape(rows_dev, feature_width)[arrange]
    listed_all = blocks.reshape(peer_count, clusters_dev * SHORT)
    owner_base = group_index * peer_count
    planner = partial(
        request_plan, owner_base=owner_base, peer_count=peer_count, per_owner=per_owner
    )
    places_all, tables_all = jax.vmap(planner)(listed_all)
    own_places = places_all[own_index].reshape(clusters_dev, SHORT)
    wanted_flat = tables_all[:, own_index, :].reshape(-1)
    block_range = jnp.arange(labels.shape[0], dtype=jnp.int32)
    reply_pick = (wanted_flat[:, None] == block_range[None, :]).astype(jnp.bfloat16)
    reply_blocks = jnp.einsum(
        "sb,bjd->sjd", reply_pick, labels, preferred_element_type=jnp.float32
    ).astype(jnp.bfloat16)
    fetched = lax.all_to_all(
        reply_blocks.reshape(peer_count, per_owner, BLK, feature_width),
        "dev",
        split_axis=0,
        concat_axis=0,
        tiled=True,
    )
    fetched = fetched.reshape(slots_total, BLK, feature_width)
    listed_ids = listed_all[own_index].reshape(clusters_dev, SHORT)
    cluster_rows = arrived.reshape(clusters_dev, CSIZE, feature_width)
    wanted_pos = positives.reshape(clusters_dev, CSIZE, NPOS)
    offsets = jnp.arange(BLK, dtype=jnp.int32)
    slot_range = jnp.arange(slots_total, dtype=jnp.int32)
    place_pick = (own_places[:, :, None] == slot_range[None, None, :]).astype(jnp.bfloat16)

    def per_cluster(running, pieces):
        rows_here, pick_here, ids_here, pos_here = pieces
        chosen = jnp.einsum(
            "ks,sjd->kjd", pick_here, fetched, preferred_element_type=jnp.float32
        ).astype(jnp.bfloat16)
        logits = jnp.einsum("qd,kjd->qkj", rows_here, chosen, preferred_element_type=jnp.float32)
        label_ids = ids_here[:, None] * BLK + offsets[None, :]
        targets = jnp.any(
            label_ids[None, :, :, None] == pos_here[:, None, None, :], axis=-1
        ).astype(jnp.float32)
        loss_rows = jnp.mean(jax.nn.softplus(logits) - targets * logits, axis=(1, 2))
        errors = (jax.nn.sigmoid(logits) - targets).astype(jnp.bfloat16)
        grad_rows = jnp.einsum(
            "qkj,kjd->qd", errors, chosen, preferred_element_type=jnp.float32
        ).astype(jnp.bfloat16)
        terms_cluster = jnp.einsum(
            "qkj,qd->kjd", errors, rows_here, preferred_element_type=jnp.float32
        )
        return (running, (loss_rows, grad_rows, terms_cluster))

    pieces = (cluster_rows, place_pick, listed_ids, wanted_pos)
    running, (losses, grads, terms) = lax.scan(per_cluster, jnp.zeros((), jnp.float32), pieces)
    selector = (own_places.reshape(-1)[:, None] == slot_range[None, :]).astype(jnp.float32)
    summed = jnp.einsum(
        "rs,rjd->sjd",
        selector,
        terms.reshape(-1, BLK, feature_width),
        precision=lax.Precision.HIGHEST,
        preferred_element_type=jnp.float32,
    )
    returned_grads = lax.all_to_all(
        summed.astype(jnp.bfloat16).reshape(peer_count, per_owner, BLK, feature_width),
        "dev",
        split_axis=0,
        concat_axis=0,
        tiled=True,
    )
    returned_grads = returned_grads.reshape(slots_total, BLK, feature_width)
    label_grad = jnp.einsum(
        "sb,sjd->bjd", reply_pick, returned_grads, preferred_element_type=jnp.float32
    ).astype(jnp.bfloat16)
    cluster_grad = grads.reshape(rows_dev, feature_width)
    returned = lax.all_to_all(
        cluster_grad[incoming].reshape(peer_count, per_peer, feature_width),
        "dev",
        split_axis=0,
        concat_axis=0,
        tiled=True,
    )
    restored = returned.reshape(rows_dev, feature_width)[jnp.argsort(outbound)]
    grad_pre = (restored.astype(jnp.float32) * activate_slope(pre_act)).astype(jnp.bfloat16)
    back_term = jnp.einsum("qe,de->qd", grad_pre, w_res, preferred_element_type=jnp.float32)
    query_grad = (restored.astype(jnp.float32) + back_term).astype(jnp.bfloat16)
    weight_term = jnp.einsum("qd,qe->de", queries, grad_pre, preferred_element_type=jnp.float32)
    weight_sum = lax.psum(weight_term, ("grp", "dev"))
    scale_factor = float(rows_dev * peer_count * groups) ** (-0.5)
    return (
        losses.reshape(rows_dev),
        query_grad,
        label_grad,
        (weight_sum * scale_factor).astype(jnp.bfloat16),
    )


def solution(mesh):
    in_specs = (
        P(("grp", "dev"), None),
        P("grp"),
        P(),
        P(("grp", "dev"), None, None),
        P("grp", None),
        P(("grp", "dev"), None),
    )
    out_specs = (P(("grp", "dev")), P(("grp", "dev"), None), P(("grp", "dev"), None, None), P())
    return jax.shard_map(local, mesh=mesh, in_specs=in_specs, out_specs=out_specs, check_vma=False)
```

profile of v0, /device:TPU:2, one launch (start us, length us, event | category | flops | bytes accessed | tf_op | source)
XLA Modules:
  0.0 643.6 jit_solution(3490546229624405968)
XLA Ops:
  8.1 3.2 sort.65
  11.2 2.6 add_convert_fusion
  13.8 1.9 gather_fusion
  15.8 11.5 %all-to-all-start = ((bf16[32,8,768]{2,1,0:T(8,128)(2,1)}), bf16[32,8,768]{2,1,0:T(8,128)(2,1)S(1)}, u32[]{:S(2)}, u32[]{:S(2)}) async-start(bf16[32,8,768]{2,1,0:T(8,128)(2,1)} %bitcast), calls=%async_computation | async-start | bytes 786432 | tf_op jit(solution)/shard_map/all_to_all | solution.py:65
  28.9 37.8 %scatter_fusion = s32[32,32]{1,0:T(8,128)S(1)} fusion(s32[32,32]{1,0:T(8,128)S(1)} %broadcast_in_dim.65, s32[768]{0:T(1024)S(1)} %reshape.324, s32[768]{0:T(1024)S(1)} %reshape.326), kind=kCustom, calls=%fused_computation.6 | custom fusion | bytes 15360 | tf_op jit(solution)/shard_map/vmap()/scatter | solution.py:37
  66.9 5.4 convert_bitcast_fusion.1
  72.3 6.3 copy.115
  78.5 10.0 %all-to-all-start.1 = ((bf16[32,1,128,768]{3,2,1,0:T(8,128)(2,1)}), bf16[32,1,128,768]{3,2,1,0:T(8,128)(2,1)}, u32[]{:S(2)}, u32[]{:S(2)}) async-start(bf16[32,1,128,768]{3,2,1,0:T(8,128)(2,1)} %copy.115), calls=%async_computation.1 | async-start | bytes 12582912 | tf_op jit(solution)/shard_map/all_to_all | solution.py:86
  91.4 5.3 gather_fusion.5
  97.9 65.0 %gather_fusion.4 = s32[8192]{0:T(1024)S(1)} fusion(s32[32,256]{1,0:T(8,128)S(1)} %reshape.266, s32[8192]{0:T(1024)S(1)} %bitcast.111), kind=kCustom, calls=%fused_computation.4 | custom fusion | bytes 131072 | tf_op jit(solution)/shard_map/jit(take_along_axis)/gather | solution.py:57
  163.3 3.2 sort.67
  167.7 60.9 %all-to-all-done.1 = bf16[32,1,128,768]{3,2,1,0:T(8,128)(2,1)} async-done(((bf16[32,1,128,768]{3,2,1,0:T(8,128)(2,1)}), bf16[32,1,128,768]{3,2,1,0:T(8,128)(2,1)}, u32[]{:S(2)}, u32[]{:S(2)}) %all-to-all-start.1) | async-done | bytes 6291488 | tf_op jit(solution)/shard_map/all_to_all | solution.py:86
  228.5 9.0 %copy.116 = bf16[32,128,768]{2,0,1:T(8,128)(2,1)} copy(bf16[32,128,768]{2,1,0:T(8,128)(2,1)} %bitcast.9) | data formatting | bytes 12582912
  237.5 22.7 %while.15 = (s32[]{:T(128)}, f32[2,128]{1,0:T(2,128)S(1)}, bf16[2,128,768]{2,1,0:T(8,128)(2,1)S(1)}, f32[2,12,128,768]{3,2,1,0:T(8,128)}, bf16[2,128,768]{2,1,0:...) while((s32[]{:T(128)}, f32[2,128]{1,0:T(2,128)S(1)}, ...), condition=%wide.region_10.11_spmd.clone, body=%wide.region_7.10_spmd.clone.sunk | while | flops 988628480 | bytes 24667932 | solution.py:122
  238.4 3.8 fusion.90
  243.7 1.6 fusion.92
  245.9 2.9 bitcast_dynamic-update-slice_fusion.2
  249.7 3.8 fusion.90
  255.0 1.6 fusion.92
  257.2 2.9 bitcast_dynamic-update-slice_fusion.2
  260.2 1.9 gather_fusion.2
  262.1 8.2 %all-to-all-start.2 = ((bf16[32,8,768]{2,1,0:T(8,128)(2,1)}), bf16[32,8,768]{2,1,0:T(8,128)(2,1)S(1)}, u32[]{:S(2)}, u32[]{:S(2)}) async-start(bf16[32,8,768]{2,1,0:T(8,128)(2,1)} %bitcast.14), calls=%async_computation.2 | async-start | bytes 786432 | tf_op jit(solution)/shard_map/all_to_all | solution.py:143
  270.3 14.7 %convert_bitcast_fusion = bf16[32,1,128,768]{3,0,2,1:T(8,128)(2,1)S(1)} fusion(f32[24,128,768]{2,1,0:T(8,128)} %bitcast.115, s32[24]{0:T(128)S(1)} %get-tuple-element.171), kind=kOutput, calls=%fused_computation.42 | convolution fusion | flops 909116160 | bytes 15728736 | tf_op jit(solution)/shard_map/rs,rjd->sjd/dot_general | solution.py:124
  285.0 6.2 copy.118
  291.3 10.2 %all-to-all-start.3 = ((bf16[32,1,128,768]{3,2,1,0:T(8,128)(2,1)}), bf16[32,1,128,768]{3,2,1,0:T(8,128)(2,1)}, u32[]{:S(2)}, u32[]{:S(2)}) async-start(bf16[32,1,128,768]{3,2,1,0:T(8,128)(2,1)} %copy.118), calls=%async_computation.3 | async-start | bytes 12582912 | tf_op jit(solution)/shard_map/all_to_all | solution.py:131
  301.7 3.2 sort.68
  306.1 2.4 convolution_bitcast_fusion.1
  308.5 1.6 fusion.33
  310.1 312.4 %all-reduce.2.cloned.1.call-done = f32[768,768]{0,1:T(8,128)} async-done(((f32[768,768]{0,1:T(8,128)}), f32[768,768]{0,1:T(8,128)}) %all-reduce.2.cloned.1.call-update) | async-done | bytes 2359312 | tf_op jit(solution)/shard_map/psum | solution.py:155
  622.6 1.8 multiply_convert_fusion
  625.9 7.9 %fusion.30 = bf16[20,128,768]{2,0,1:T(8,128)(2,1)S(1)} fusion(bf16[32,1,128,768]{3,2,1,0:T(8,128)(2,1)} %all-to-all-done.3, s32[32]{0:T(128)S(1)} %dynamic-slice_reduce_fusion), kind=kOutput, calls=%fused_computation.46 | convolution fusion | flops 127795840 | bytes 10223744 | tf_op jit(solution)/shard_map/sb,sjd->bjd/dot_general | solution.py:139
  633.8 2.8 copy.120
  (104 shorter events, 17.0 us)
Async XLA Ops:
  7.2 4.1 copy-start
  7.2 20.1 %copy-start.2 = (s32[64,12]{0,1:T(8,128)S(1)}, s32[64,12]{0,1:T(8,128)}, u32[]{:S(2)}) copy-start(s32[64,12]{0,1:T(8,128)} %param.12) | copy-start | bytes 9220
  15.8 62.8 %all-to-all-start = ((bf16[32,8,768]{2,1,0:T(8,128)(2,1)}), bf16[32,8,768]{2,1,0:T(8,128)(2,1)S(1)}, u32[]{:S(2)}, u32[]{:S(2)}) async-start(bf16[32,8,768]{2,1,0:T(8,128)(2,1)} %bitcast), calls=%async_computation | async-start | bytes 786432 | tf_op jit(solution)/shard_map/all_to_all | solution.py:65
  78.5 10.1 %copy-start.3 = (s32[8192]{0:T(1024)S(1)}, s32[8192]{0:T(1024)}, u32[]{:S(2)}) copy-start(s32[8192]{0:T(1024)} %param.9) | copy-start | bytes 98308
  78.5 150.0 %all-to-all-start.1 = ((bf16[32,1,128,768]{3,2,1,0:T(8,128)(2,1)}), bf16[32,1,128,768]{3,2,1,0:T(8,128)(2,1)}, u32[]{:S(2)}, u32[]{:S(2)}) async-start(bf16[32,1,128,768]{3,2,1,0:T(8,128)(2,1)} %copy.115), calls=%async_computation.1 | async-start | bytes 12582912 | tf_op jit(solution)/shard_map/all_to_all | solution.py:86
  88.6 8.5 %sort.70.cloned.1.call-start = ((), (), s32[]{:S(2)}) async-start(), calls=%async_computation.5 | async-start | bytes 196640 | tf_op jit(solution)/shard_map/jit(argsort)/sort | solution.py:56
  97.9 65.0 %copy-start.1 = (s32[32,256]{1,0:T(8,128)S(1)}, s32[32,256]{1,0:T(8,128)}, u32[]{:S(2)}) copy-start(s32[32,256]{1,0:T(8,128)} %get-tuple-element.64) | copy-start | bytes 98308
  228.5 9.0 %copy-start.4 = (s32[256,4]{0,1:T(4,128)S(1)}, s32[256,4]{0,1:T(4,128)}, u32[]{:S(2)}) copy-start(s32[256,4]{0,1:T(4,128)} %param.13) | copy-start | bytes 12292
  260.2 24.9 %copy-start.6 = (f32[2,128]{1,0:T(2,128)}, f32[2,128]{1,0:T(2,128)S(1)}, u32[]{:S(2)}) copy-start(f32[2,128]{1,0:T(2,128)S(1)} %get-tuple-element.67) | copy-start | bytes 3076
  262.1 29.2 %all-to-all-start.2 = ((bf16[32,8,768]{2,1,0:T(8,128)(2,1)}), bf16[32,8,768]{2,1,0:T(8,128)(2,1)S(1)}, u32[]{:S(2)}, u32[]{:S(2)}) async-start(bf16[32,8,768]{2,1,0:T(8,128)(2,1)} %bitcast.14), calls=%async_computation.2 | async-start | bytes 786432 | tf_op jit(solution)/shard_map/all_to_all | solution.py:143
  291.3 14.8 %copy-start.5 = (bf16[256,768]{1,0:T(8,128)(2,1)S(1)}, bf16[256,768]{1,0:T(8,128)(2,1)}, u32[]{:S(2)}) copy-start(bf16[256,768]{1,0:T(8,128)(2,1)} %param.8) | copy-start | bytes 1179652
  291.3 14.8 %copy-start.7 = (f32[256,768]{1,0:T(8,128)S(1)}, f32[256,768]{1,0:T(8,128)}, u32[]{:S(2)}) copy-start(f32[256,768]{1,0:T(8,128)} %get-tuple-element.176) | copy-start | bytes 2359300
  291.3 334.6 %all-to-all-start.3 = ((bf16[32,1,128,768]{3,2,1,0:T(8,128)(2,1)}), bf16[32,1,128,768]{3,2,1,0:T(8,128)(2,1)}, u32[]{:S(2)}, u32[]{:S(2)}) async-start(bf16[32,1,128,768]{3,2,1,0:T(8,128)(2,1)} %copy.118), calls=%async_computation.3 | async-start | bytes 12582912 | tf_op jit(solution)/shard_map/all_to_all | solution.py:131
  301.4 321.1 %all-reduce.2.cloned.1.call-start = ((), (), s32[]{:S(2)}) async-start(), calls=%async_computation.4 | async-start | bytes 4718592 | tf_op jit(solution)/shard_map/psum | solution.py:155
Sparse Core Ops, SparseCore 0:
  92.3 2.5 sort.72.cloned.1.call-done
  308.6 313.9 all-reduce.1
  (1 shorter events, 0.0 us)
where the time goes:
time: 652 us; the launch traced here: 644 us
  waiting for transfers between devices  373 us (57%)
  local copies, waits for them, and re-layouts  143 us (22%)
  matrix products  54.2 us (8%)
  starting transfers between devices  40.1 us (6%)
  other arithmetic  17.9 us (3%)
  between operations  14.6 us (2%)
    psum x1, waiting for transfers between devices, local(): weight_sum = lax.psum(weight_term, ('grp', 'dev'))  312 us
    gather x2, local copies, waits for them, and re-layouts, local(): grid_sorted = jnp.take_along_axis(slot_grid, grid_order, axis=1)  65 us
    all_to_all x1, waiting for transfers between devices, local(): lax.all_to_all(reply_blocks.reshape(peer_count, per_owner, BLK, feature_w...  60.9 us
    scatter x3, local copies, waits for them, and re-layouts, request_plan(): jnp.full((peer_count * per_owner,), -1, jnp.int32).at[target]  38 us
    dot_general x1, matrix products, local(): jnp.einsum('rs,rjd->sjd', selector, terms.reshape(-1, BLK, feature_width)...  14.7 us
    unnamed x22, local copies, waits for them, and re-layouts  13.4 us
  transfers between devices with their start and end apart: 5, of which 2 were waited for; matrix products, arithmetic and copies ran while one was open for 25% of the time, Pallas kernels for 0%

commit v1 on v0

--- a/solution.py
+++ b/solution.py
@@ -152,7 +152,7 @@
     back_term = jnp.einsum("qe,de->qd", grad_pre, w_res, preferred_element_type=jnp.float32)
     query_grad = (restored.astype(jnp.float32) + back_term).astype(jnp.bfloat16)
     weight_term = jnp.einsum("qd,qe->de", queries, grad_pre, preferred_element_type=jnp.float32)
-    weight_sum = lax.psum(weight_term, ("grp", "dev"))
+    weight_sum = lax.psum(lax.psum(weight_term, "grp"), "dev")
     scale_factor = float(rows_dev * peer_count * groups) ** (-0.5)
     return (
         losses.reshape(rows_dev),

time: 652 us -> 603 us (0.925)
  waiting for transfers between devices: 373 us -> 325 us
    psum x1 -> x2, waiting for transfers between devices: 312 us -> 264 us  [local(): weight_sum = lax.psum(lax.psum(weight_term, 'grp'), 'dev')]
  transfers between devices with their start and end apart: 5 -> 6, of which waited for: 2 -> 3; matrix products, arithmetic and copies ran while one was open for 25% -> 27% of each run, Pallas kernels for 0% -> 0%
where the time goes in v1:
time: 603 us; the launch traced here: 595 us
  waiting for transfers between devices  325 us (54%)
  local copies, waits for them, and re-layouts  143 us (24%)
  matrix products  54.2 us (9%)
  starting transfers between devices  40.2 us (7%)
  other arithmetic  17.9 us (3%)
  between operations  14.3 us (2%)
    psum x2, waiting for transfers between devices, local(): weight_sum = lax.psum(lax.psum(weight_term, 'grp'), 'dev')  264 us
    gather x2, local copies, waits for them, and re-layouts, local(): grid_sorted = jnp.take_along_axis(slot_grid, grid_order, axis=1)  65 us
    all_to_all x1, waiting for transfers between devices, local(): lax.all_to_all(reply_blocks.reshape(peer_count, per_owner, BLK, feature_w...  60.9 us
    scatter x3, local copies, waits for them, and re-layouts, request_plan(): jnp.full((peer_count * per_owner,), -1, jnp.int32).at[target]  38 us
    dot_general x1, matrix products, local(): jnp.einsum('rs,rjd->sjd', selector, terms.reshape(-1, BLK, feature_width)...  14.7 us
    unnamed x22, local copies, waits for them, and re-layouts  13.4 us
  transfers between devices with their start and end apart: 6, of which 3 were waited for; matrix products, arithmetic and copies ran while one was open for 27% of the time, Pallas kernels for 0%

profile of v1, /device:TPU:2, one launch (start us, length us, event | category | flops | bytes accessed | tf_op | source)
XLA Modules:
  0.0 595.1 jit_solution(5964970896359810605)
XLA Ops:
  8.1 3.2 sort.65
  11.2 2.6 add_convert_fusion
  13.8 1.9 gather_fusion
  15.8 11.5 %all-to-all-start = ((bf16[32,8,768]{2,1,0:T(8,128)(2,1)}), bf16[32,8,768]{2,1,0:T(8,128)(2,1)S(1)}, u32[]{:S(2)}, u32[]{:S(2)}) async-start(bf16[32,8,768]{2,1,0:T(8,128)(2,1)} %bitcast), calls=%async_computation | async-start | bytes 786432 | tf_op jit(solution)/shard_map/all_to_all | solution.py:65
  28.9 37.8 %scatter_fusion = s32[32,32]{1,0:T(8,128)S(1)} fusion(s32[32,32]{1,0:T(8,128)S(1)} %broadcast_in_dim.65, s32[768]{0:T(1024)S(1)} %reshape.324, s32[768]{0:T(1024)S(1)} %reshape.326), kind=kCustom, calls=%fused_computation.6 | custom fusion | bytes 15360 | tf_op jit(solution)/shard_map/vmap()/scatter | solution.py:37
  66.9 5.4 convert_bitcast_fusion.1
  72.3 6.3 %copy.115 = bf16[32,1,128,768]{3,2,1,0:T(8,128)(2,1)} copy(bf16[32,1,128,768]{3,0,2,1:T(8,128)(2,1)S(1)} %convert_bitcast_fusion.1) | data formatting | bytes 12582912 | tf_op jit(solution)/shard_map/reshape | solution.py:87
  78.5 10.0 %all-to-all-start.1 = ((bf16[32,1,128,768]{3,2,1,0:T(8,128)(2,1)}), bf16[32,1,128,768]{3,2,1,0:T(8,128)(2,1)}, u32[]{:S(2)}, u32[]{:S(2)}) async-start(bf16[32,1,128,768]{3,2,1,0:T(8,128)(2,1)} %copy.115), calls=%async_computation.1 | async-start | bytes 12582912 | tf_op jit(solution)/shard_map/all_to_all | solution.py:86
  91.4 5.3 gather_fusion.5
  97.9 65.0 %gather_fusion.4 = s32[8192]{0:T(1024)S(1)} fusion(s32[32,256]{1,0:T(8,128)S(1)} %reshape.266, s32[8192]{0:T(1024)S(1)} %bitcast.111), kind=kCustom, calls=%fused_computation.4 | custom fusion | bytes 131072 | tf_op jit(solution)/shard_map/jit(take_along_axis)/gather | solution.py:57
  163.3 3.2 sort.67
  167.7 60.9 %all-to-all-done.1 = bf16[32,1,128,768]{3,2,1,0:T(8,128)(2,1)} async-done(((bf16[32,1,128,768]{3,2,1,0:T(8,128)(2,1)}), bf16[32,1,128,768]{3,2,1,0:T(8,128)(2,1)}, u32[]{:S(2)}, u32[]{:S(2)}) %all-to-all-start.1) | async-done | bytes 6291488 | tf_op jit(solution)/shard_map/all_to_all | solution.py:86
  228.5 9.0 %copy.116 = bf16[32,128,768]{2,0,1:T(8,128)(2,1)} copy(bf16[32,128,768]{2,1,0:T(8,128)(2,1)} %bitcast.9) | data formatting | bytes 12582912
  237.5 22.7 %while.15 = (s32[]{:T(128)}, f32[2,128]{1,0:T(2,128)S(1)}, bf16[2,128,768]{2,1,0:T(8,128)(2,1)S(1)}, f32[2,12,128,768]{3,2,1,0:T(8,128)}, bf16[2,128,768]{2,1,0:...) while((s32[]{:T(128)}, f32[2,128]{1,0:T(2,128)S(1)}, ...), condition=%wide.region_10.11_spmd.clone, body=%wide.region_7.10_spmd.clone.sunk | while | flops 988628480 | bytes 24667932 | solution.py:122
  238.4 3.8 fusion.90
  245.9 2.9 bitcast_dynamic-update-slice_fusion.2
  249.7 3.8 fusion.90
  255.0 1.6 fusion.92
  257.2 2.9 bitcast_dynamic-update-slice_fusion.2
  260.2 1.9 gather_fusion.2
  262.1 8.2 %all-to-all-start.2 = ((bf16[32,8,768]{2,1,0:T(8,128)(2,1)}), bf16[32,8,768]{2,1,0:T(8,128)(2,1)S(1)}, u32[]{:S(2)}, u32[]{:S(2)}) async-start(bf16[32,8,768]{2,1,0:T(8,128)(2,1)} %bitcast.14), calls=%async_computation.2 | async-start | bytes 786432 | tf_op jit(solution)/shard_map/all_to_all | solution.py:143
  270.3 14.7 %convert_bitcast_fusion = bf16[32,1,128,768]{3,0,2,1:T(8,128)(2,1)S(1)} fusion(f32[24,128,768]{2,1,0:T(8,128)} %bitcast.115, s32[24]{0:T(128)S(1)} %get-tuple-element.171), kind=kOutput, calls=%fused_computation.42 | convolution fusion | flops 909116160 | bytes 15728736 | tf_op jit(solution)/shard_map/rs,rjd->sjd/dot_general | solution.py:124
  285.0 6.2 %copy.118 = bf16[32,1,128,768]{3,2,1,0:T(8,128)(2,1)} copy(bf16[32,1,128,768]{3,0,2,1:T(8,128)(2,1)S(1)} %convert_bitcast_fusion) | data formatting | bytes 12582912 | tf_op jit(solution)/shard_map/reshape | solution.py:132
  291.3 10.2 %all-to-all-start.3 = ((bf16[32,1,128,768]{3,2,1,0:T(8,128)(2,1)}), bf16[32,1,128,768]{3,2,1,0:T(8,128)(2,1)}, u32[]{:S(2)}, u32[]{:S(2)}) async-start(bf16[32,1,128,768]{3,2,1,0:T(8,128)(2,1)} %copy.118), calls=%async_computation.3 | async-start | bytes 12582912 | tf_op jit(solution)/shard_map/all_to_all | solution.py:131
  301.7 3.2 sort.68
  306.1 2.4 convolution_bitcast_fusion.1
  308.5 72.1 %all-reduce.3.cloned.1.call-done = f32[768,768]{0,1:T(8,128)} async-done(((f32[768,768]{0,1:T(8,128)}), f32[768,768]{0,1:T(8,128)}) %all-reduce.3.cloned.1.call-update) | async-done | bytes 2359312 | tf_op jit(solution)/shard_map/psum | solution.py:155
  380.7 1.6 fusion.33
  382.3 192.0 %all-reduce.5.cloned.1.call-done = f32[768,768]{0,1:T(8,128)} async-done(((f32[768,768]{0,1:T(8,128)}), f32[768,768]{0,1:T(8,128)}) %all-reduce.5.cloned.1.call-update) | async-done | bytes 2359312 | tf_op jit(solution)/shard_map/psum | solution.py:155
  574.3 1.8 multiply_convert_fusion
  577.6 7.9 %fusion.30 = bf16[20,128,768]{2,0,1:T(8,128)(2,1)S(1)} fusion(bf16[32,1,128,768]{3,2,1,0:T(8,128)(2,1)} %all-to-all-done.3, s32[32]{0:T(128)S(1)} %dynamic-slice_reduce_fusion), kind=kOutput, calls=%fused_computation.46 | convolution fusion | flops 127795840 | bytes 10223744 | tf_op jit(solution)/shard_map/sb,sjd->bjd/dot_general | solution.py:139
  585.5 2.8 copy.120
  (107 shorter events, 18.6 us)
Async XLA Ops:
  7.2 4.1 copy-start
  7.2 20.1 %copy-start.2 = (s32[64,12]{0,1:T(8,128)S(1)}, s32[64,12]{0,1:T(8,128)}, u32[]{:S(2)}) copy-start(s32[64,12]{0,1:T(8,128)} %param.12) | copy-start | bytes 9220
  15.8 62.8 %all-to-all-start = ((bf16[32,8,768]{2,1,0:T(8,128)(2,1)}), bf16[32,8,768]{2,1,0:T(8,128)(2,1)S(1)}, u32[]{:S(2)}, u32[]{:S(2)}) async-start(bf16[32,8,768]{2,1,0:T(8,128)(2,1)} %bitcast), calls=%async_computation | async-start | bytes 786432 | tf_op jit(solution)/shard_map/all_to_all | solution.py:65
  78.5 10.1 %copy-start.3 = (s32[8192]{0:T(1024)S(1)}, s32[8192]{0:T(1024)}, u32[]{:S(2)}) copy-start(s32[8192]{0:T(1024)} %param.9) | copy-start | bytes 98308
  78.5 150.0 %all-to-all-start.1 = ((bf16[32,1,128,768]{3,2,1,0:T(8,128)(2,1)}), bf16[32,1,128,768]{3,2,1,0:T(8,128)(2,1)}, u32[]{:S(2)}, u32[]{:S(2)}) async-start(bf16[32,1,128,768]{3,2,1,0:T(8,128)(2,1)} %copy.115), calls=%async_computation.1 | async-start | bytes 12582912 | tf_op jit(solution)/shard_map/all_to_all | solution.py:86
  88.6 8.5 %sort.70.cloned.1.call-start = ((), (), s32[]{:S(2)}) async-start(), calls=%async_computation.6 | async-start | bytes 196640 | tf_op jit(solution)/shard_map/jit(argsort)/sort | solution.py:56
  97.9 65.0 %copy-start.1 = (s32[32,256]{1,0:T(8,128)S(1)}, s32[32,256]{1,0:T(8,128)}, u32[]{:S(2)}) copy-start(s32[32,256]{1,0:T(8,128)} %get-tuple-element.64) | copy-start | bytes 98308
  228.5 9.0 %copy-start.4 = (s32[256,4]{0,1:T(4,128)S(1)}, s32[256,4]{0,1:T(4,128)}, u32[]{:S(2)}) copy-start(s32[256,4]{0,1:T(4,128)} %param.13) | copy-start | bytes 12292
  260.2 24.9 %copy-start.6 = (f32[2,128]{1,0:T(2,128)}, f32[2,128]{1,0:T(2,128)S(1)}, u32[]{:S(2)}) copy-start(f32[2,128]{1,0:T(2,128)S(1)} %get-tuple-element.67) | copy-start | bytes 3076
  262.1 29.2 %all-to-all-start.2 = ((bf16[32,8,768]{2,1,0:T(8,128)(2,1)}), bf16[32,8,768]{2,1,0:T(8,128)(2,1)S(1)}, u32[]{:S(2)}, u32[]{:S(2)}) async-start(bf16[32,8,768]{2,1,0:T(8,128)(2,1)} %bitcast.14), calls=%async_computation.2 | async-start | bytes 786432 | tf_op jit(solution)/shard_map/all_to_all | solution.py:143
  291.3 14.8 %copy-start.5 = (bf16[256,768]{1,0:T(8,128)(2,1)S(1)}, bf16[256,768]{1,0:T(8,128)(2,1)}, u32[]{:S(2)}) copy-start(bf16[256,768]{1,0:T(8,128)(2,1)} %param.8) | copy-start | bytes 1179652
  291.3 14.8 %copy-start.7 = (f32[256,768]{1,0:T(8,128)S(1)}, f32[256,768]{1,0:T(8,128)}, u32[]{:S(2)}) copy-start(f32[256,768]{1,0:T(8,128)} %get-tuple-element.176) | copy-start | bytes 2359300
  291.3 286.4 %all-to-all-start.3 = ((bf16[32,1,128,768]{3,2,1,0:T(8,128)(2,1)}), bf16[32,1,128,768]{3,2,1,0:T(8,128)(2,1)}, u32[]{:S(2)}, u32[]{:S(2)}) async-start(bf16[32,1,128,768]{3,2,1,0:T(8,128)(2,1)} %copy.118), calls=%async_computation.3 | async-start | bytes 12582912 | tf_op jit(solution)/shard_map/all_to_all | solution.py:131
  301.4 79.2 %all-reduce.3.cloned.1.call-start = ((), (), s32[]{:S(2)}) async-start(), calls=%async_computation.4 | async-start | bytes 4718592 | tf_op jit(solution)/shard_map/psum | solution.py:155
  308.5 265.9 %all-reduce.5.cloned.1.call-start = ((), (), s32[]{:S(2)}) async-start(), calls=%async_computation.5 | async-start | bytes 4718592 | tf_op jit(solution)/shard_map/psum | solution.py:155
Sparse Core Ops, SparseCore 0:
  92.3 2.5 sort.72.cloned.1.call-done
  308.6 71.9 all-reduce.2
  384.2 190.1 all-reduce.4
  (1 shorter events, 0.0 us)
